TPU v7x, 256 devices: a whole 4x4x8 slice. The times are simulated.
256 devices in a mesh: section: 4 (over y), chan: 64 (over x, z, core).
Axes of the slice: x: 4, y: 4, z: 8, core: 2. Of those that a mesh axis runs over, the one named last changes fastest.
Arguments:
- voltages: bfloat16 [2, 1024, 16, 4096], P(None, 'chan', 'section'), may hold values from -6 to 6
- coefficients: float32 [4, 4096], replicated, may hold values from -0.046875 to 0.046875
- tile_order: int32 [64, 36], P('chan'), may hold values from 0 to 35, each once within a row
- steer_table: bfloat16 [256, 2, 512], replicated, may hold values from -0.1875 to 0.1875
- beam_index: int32 [256, 64], P(None, 'chan'), may hold values from 0 to 255
Outputs:
- visibility: float32 [64, 36, 2, 128, 128], P('chan', 'section')
- beam_power: float32 [2, 256, 16, 4096], P(None, None, 'section', 'chan')
Inputs may be any that keep to these rules, and one draw needn't show every extreme that they name: Row g of tile_order lists each of the 36 work items of channel column g exactly once.
All inputs are finite; a program needn't handle non-finite values.
Results may differ from a plain program's by a relative error of at most 0.0029.
Values may be sent and summed in bfloat16 or wider, within the bound.
A program may use at most 64 MiB of HBM per device.

v0:
```python
import math
import jax
import jax.numpy as jnp
from jax import lax
from jax.sharding import PartitionSpec as P

STATIONS = 512
INPUTS = 1024
NA = 64
NB = 64
AVG = 64
TB = 128
PAIRS = 36
NBEAM = 256


def shifted(value, axis, by):
    devices = lax.axis_size(axis)
    pairs = [(i, i + by) for i in range(devices) if 0 <= i + by < devices]
    return lax.ppermute(value, axis, pairs)


def dft_table(length):
    counter = lax.iota(jnp.int32, length)
    phases = counter[:, None] * counter[None, :] % length
    angles = 2.0 * math.pi / length * phases.astype(jnp.float32)
    cosine = jnp.cos(angles)
    sine_part = jnp.sin(angles)
    return jnp.stack([jnp.stack([cosine, -sine_part]), jnp.stack([sine_part, cosine])])


def channelize(filtered):
    spectra_count = filtered.shape[1]
    length = NA * NB
    blocks = filtered.reshape(2, spectra_count, NA, NB)
    section_one = jnp.einsum("qmab,qrac->rmcb", blocks, dft_table(NA), precision=lax.Precision.HIGH)
    row_index = lax.iota(jnp.int32, NA)
    col_index = lax.iota(jnp.int32, NB)
    angles = (
        2.0
        * math.pi
        / length
        * (row_index[:, None] * col_index[None, :] % length).astype(jnp.float32)
    )
    cosine = jnp.cos(angles)
    sine_part = jnp.sin(angles)
    turned_real = section_one[0] * cosine + section_one[1] * sine_part
    turned_imag = section_one[1] * cosine - section_one[0] * sine_part
    twisted = jnp.stack([turned_real, turned_imag])
    section_two = jnp.einsum(
        "rmcb,rsbd->smdc", twisted, dft_table(NB), precision=lax.Precision.HIGH
    )
    return section_two.reshape(2, spectra_count, length)


def pair_products(spectra, work_items):
    tile_count = INPUTS // TB
    local_channel = work_items // PAIRS
    pair_number = work_items % PAIRS
    tile_ids = lax.iota(jnp.int32, tile_count)
    first_pairs = tile_ids * (tile_ids + 1) // 2
    row_tiles = (
        jnp.sum((first_pairs[None, :] <= pair_number[:, None]).astype(jnp.int32), axis=1) - 1
    )
    col_tiles = pair_number - row_tiles * (row_tiles + 1) // 2
    frame_count = spectra.shape[2]
    channel_groups = spectra.shape[3] // AVG
    blocks = spectra.reshape(2, tile_count, TB, frame_count, channel_groups, AVG)
    tile_table = jnp.transpose(blocks, (1, 4, 0, 2, 3, 5)).reshape(
        tile_count * channel_groups, 2, TB, frame_count * AVG
    )
    row_block = jnp.take(tile_table, row_tiles * channel_groups + local_channel, axis=0)
    col_block = jnp.take(tile_table, col_tiles * channel_groups + local_channel, axis=0)
    swapped = jnp.stack([row_block[:, 1], -row_block[:, 0]], axis=1)
    numbers = (((1, 3), (1, 3)), ((0,), (0,)))
    real_part = lax.dot_general(row_block, col_block, numbers, preferred_element_type=jnp.float32)
    imag_part = lax.dot_general(swapped, col_block, numbers, preferred_element_type=jnp.float32)
    return jnp.stack([real_part, imag_part], axis=1)


def shards(voltages, coefficients, tile_order, steer_table, beam_index):
    section_count = lax.axis_size("section")
    inputs_dev = voltages.shape[1]
    frames_dev = voltages.shape[2]
    tap_count = coefficients.shape[0]
    history = shifted(voltages[:, :, frames_dev - (tap_count - 1) :, :], "section", 1)
    extended = jnp.concatenate([history, voltages], axis=2).astype(jnp.float32)
    filtered = jnp.zeros(voltages.shape, jnp.float32)
    for tap_index in range(tap_count):
        offset = tap_count - 1 - tap_index
        filtered = (
            filtered + coefficients[tap_index] * extended[:, :, offset : offset + frames_dev, :]
        )
    spectra = (
        channelize(filtered.reshape(2, inputs_dev * frames_dev, NA * NB))
        .reshape(voltages.shape)
        .astype(jnp.bfloat16)
    )
    weights = steer_table[beam_index]
    out_dev = beam_index.shape[1]
    shard_piece = lax.all_to_all(spectra, "chan", split_axis=3, concat_axis=1, tiled=True)
    frame_count = shard_piece.shape[2]
    grouped = shard_piece.reshape(2, STATIONS, 2, frame_count, out_dev, AVG)
    product = lax.dot_general(
        weights, grouped, (((3,), (1,)), ((1,), (4,))), preferred_element_type=jnp.float32
    )
    real_part = product[:, :, 0, 0] - product[:, :, 1, 1]
    imag_part = product[:, :, 0, 1] + product[:, :, 1, 0]
    beam_energy = real_part * real_part + imag_part * imag_part
    beam_power = jnp.transpose(beam_energy, (2, 1, 3, 0, 4)).reshape(
        2, NBEAM, frame_count, out_dev * AVG
    )
    column_items = tile_order[0]
    items_dev = column_items.shape[0] // section_count
    mean_factor = 1.0 / (frames_dev * section_count * AVG)
    own_items = lax.dynamic_slice_in_dim(
        column_items, lax.axis_index("section") * items_dev, items_dev
    )
    totals = pair_products(lax.all_gather(shard_piece, "section", axis=2, tiled=True), own_items)
    visibility = (totals * mean_factor)[None]
    return (visibility, beam_power)


def solution(mesh):
    placed = (P(None, "chan", "section", None), P(), P("chan", None), P(), P(None, "chan"))
    return jax.shard_map(
        shards,
        mesh=mesh,
        in_specs=placed,
        out_specs=(P("chan", "section", None, None, None), P(None, None, "section", "chan")),
        check_vma=False,
    )
```

profile of v0, /device:TPU:1, one launch (start us, length us, event | category | flops | bytes accessed | tf_op | source)
XLA Modules:
  0.0 257.8 jit_solution(14299678543089905093)
XLA Ops:
  7.2 1.9 slice.54
  9.2 0.6 copy.79
  9.7 4.1 %collective-permute-start = (bf16[2,16,3,4096]{3,1,2,0:T(8,128)(2,1)S(1)}, bf16[2,16,3,4096]{3,1,2,0:T(8,128)(2,1)S(1)}, u32[]{:S(2)}, u32[]{:S(2)}) collective-permute-start(bf16[2,16,3,4096]{3,1,2,0:T(8,128)(2,1)S(1)} %copy.79), channel_id=1, source_target_pairs={{0,64},{64,128},{128,192},{1,65},{65,129},{129,193},{2,66},{66,130... | collective-permute-start | bytes 2359304 | tf_op jit(solution)/shard_map/ppermute | solution.py:20
  14.4 15.6 %collective-permute-done = bf16[2,16,3,4096]{3,1,2,0:T(8,128)(2,1)S(1)} collective-permute-done((bf16[2,16,3,4096]{3,1,2,0:T(8,128)(2,1)S(1)}, bf16[2,16,3,4096]{3,1,2,0:T(8,128)(2,1)S(1)}, u32[]{:S(2)}, u32[]{:S(2)}) %collective-permute-start) | collective-permute-done | bytes 786464 | tf_op jit(solution)/shard_map/ppermute | solution.py:20
  30.0 0.7 copy.52
  30.7 1.0 maximum_convert_fusion
  31.7 1.8 fusion.14
  33.5 3.3 %reshape_reshape.4 = f32[2,64,64,64]{3,2,1,0:T(8,128)} reshape(f32[2,16,4,4096]{3,2,1,0:T(4,128)S(1)} %fusion.14) | data formatting | bytes 4194304 | tf_op jit(solution)/shard_map/reshape;reshape | solution.py:35
  36.9 4.2 %fusion.10 = f32[2,64,64,64]{3,2,1,0:T(8,128)S(1)} fusion(f32[2,64,64,64]{3,2,1,0:T(8,128)} %reshape_reshape.4, f32[1,2,64,64]{2,3,0,1:T(8,128)S(1)} %get-tuple-element.27, f32[1,2,64,64]{2,3,0,1:T(8,128)S(1)} %get-tuple-element.26), kind=kOutput, calls=%fused_computation.18 | convolution fusion | flops 402669568 | bytes 4259840 | tf_op jit(solution)/shard_map/qmab,qrac->rmcb/dot_general | solution.py:36
  41.0 1.0 multiply_add_fusion
  42.0 3.3 %fusion.13 = bf16[2,64,64,64]{3,2,1,0:T(8,128)(2,1)S(1)} fusion(f32[1,2,64,64]{2,3,0,1:T(8,128)S(1)} %get-tuple-element.27, f32[1,2,64,64]{2,3,0,1:T(8,128)S(1)} %get-tuple-element.26, f32[1,64,64,64]{3,2,1,0:T(8,128)S(1)} %get-tuple-element.21, f32[1,64,64,64]{3,2,1,0:T(8,128)S(1)} %get-tuple-element.20), kind=kOutput, calls=%fused_computation.19 | convolution fusion | flops 403718144 | bytes 3211264 | tf_op jit(solution)/shard_map/rmcb,rsbd->smdc/dot_general | solution.py:50
  45.3 2.2 convert_element_type.61
  47.5 12.0 %copy.55 = bf16[2,16,4,4096]{1,2,0,3:T(4,128)(2,1)} copy(bf16[2,16,4,4096]{3,2,1,0:T(4,128)(2,1)} %convert_element_type.61) | data formatting | bytes 2097152 | tf_op jit(solution)/shard_map/convert_element_type | solution.py:97
  59.5 11.9 %reshape.317 = bf16[64,2,4096]{2,1,0:T(2,128)(2,1)S(1)} reshape(bf16[4096,2,4,16]{3,2,1,0:T(4,128)(2,1)} %bitcast.95) | data formatting | bytes 2097152
  71.4 41.3 %all_to_all.18 = bf16[64,2,4096]{2,1,0:T(2,128)(2,1)S(1)} all-to-all(bf16[64,2,4096]{2,1,0:T(2,128)(2,1)S(1)} %reshape.317), channel_id=1, replica_groups=mesh['section'=4,'chan'=64] {'chan'}, dimensions={0} | all-to-all | bytes 2097152 | tf_op jit(solution)/shard_map/all_to_all | solution.py:101
  112.7 7.5 %reshape.318 = bf16[4096,2,4,16]{3,2,1,0:T(4,128)(2,1)} reshape(bf16[64,2,4096]{2,1,0:T(2,128)(2,1)S(1)} %all_to_all.18) | data formatting | bytes 2097152
  120.3 11.4 %copy.75 = bf16[2,16,4,64,64]{4,1,3,2,0:T(8,128)(2,1)} copy(bf16[2,16,4,64,64]{1,2,0,4,3:T(4,128)(2,1)} %bitcast.94) | data formatting | bytes 2097152 | tf_op jit(solution)/shard_map/all_to_all | solution.py:101
  131.7 1.7 gather_fusion
  133.9 3.5 %copy.64 = bf16[2,512,2,4,64]{1,4,3,2,0:T(8,128)(2,1)} copy(bf16[2,512,2,4,64]{4,2,1,3,0:T(2,128)(2,1)S(1)} %bitcast.97) | data formatting | bytes 2097152 | tf_op jit(solution)/shard_map/reshape.8
  137.4 2.0 convolution_bitcast_fusion
  139.4 1.0 fusion.27
  140.3 74.9 %all-gather.2.cloned.1.call-done = bf16[2,1024,16,64]{3,1,2,0:T(8,128)(2,1)} async-done(((bf16[2,1024,4,64]{3,1,2,0:T(8,128)(2,1)}), bf16[2,1024,16,64]{3,1,2,0:T(8,128)(2,1)}) %all-gather.2.cloned.1.call-update) | async-done | bytes 4194320 | tf_op jit(solution)/shard_map/all_gather | solution.py:119
  215.2 8.6 %copy.58 = bf16[2,8,128,16,1,64]{2,5,3,0,1,4:T(8,128)(2,1)} copy(bf16[2,8,128,16,1,64]{5,2,1,3,0,4:T(8,128)(2,1)} %bitcast.98) | data formatting | bytes 8388608 | tf_op jit(solution)/shard_map/reshape | solution.py:68
  223.8 6.5 %copy.59 = bf16[8,2,128,1024]{3,2,1,0:T(8,128)(2,1)} copy(bf16[8,2,128,1024]{2,3,1,0:T(8,128)(2,1)} %bitcast.92) | data formatting | bytes 8388608 | tf_op jit(solution)/shard_map/reshape | solution.py:69
  230.3 5.8 %gather_fusion.2 = bf16[9,2,128,1024]{2,3,1,0:T(8,128)(2,1)} fusion(bf16[8,2,128,1024]{2,3,1,0:T(8,128)(2,1)} %bitcast.93, s32[1024]{0:T(1024)S(1)} %pad_clamp_fusion.1), kind=kCustom, calls=%fused_computation.1.clone | custom fusion | bytes 9437220 | tf_op jit(solution)/shard_map/jit(_take)/gather | solution.py:73
  236.1 5.8 %gather_fusion.1 = bf16[9,2,128,1024]{3,2,1,0:T(8,128)(2,1)} fusion(bf16[8,2,128,1024]{3,2,1,0:T(8,128)(2,1)} %copy.59, s32[1024]{0:T(1024)S(1)} %pad_clamp_fusion.2), kind=kCustom, calls=%fused_computation.clone | custom fusion | bytes 9437220 | tf_op jit(solution)/shard_map/jit(_take)/gather | solution.py:72
  242.0 3.0 %broadcast_select_fusion.1 = bf16[9,2,128,1024]{3,2,1,0:T(8,128)(2,1)S(1)} fusion(bf16[9,2,128,1024]{3,2,1,0:T(8,128)(2,1)} %gather_fusion.1, pred[9]{0:T(512)(128)(4,1)S(1)} %get-tuple-element.13), kind=kLoop, calls=%fused_computation.8 | loop fusion | flops 2359296 | bytes 9437193 | tf_op jit(solution)/shard_map/jit(_take)/select_n | solution.py:72
  245.0 0.3 fusion.54
  245.6 0.6 slice-done.1
  246.2 1.5 fusion.20
  247.6 2.0 fusion.21
  249.8 1.1 copy.65
  (35 shorter events, 1.4 us)
Async XLA Ops:
  7.2 124.6 %copy-start = (bf16[256,2,512]{2,1,0:T(2,128)(2,1)S(1)}, bf16[256,2,512]{2,1,0:T(2,128)(2,1)}, u32[]{:S(2)}) copy-start(bf16[256,2,512]{2,1,0:T(2,128)(2,1)} %param.10) | copy-start | bytes 1572868
  7.2 7.1 %copy-start.4 = (f32[4,4096]{1,0:T(4,128)S(1)}, f32[4,4096]{1,0:T(4,128)}, u32[]{:S(2)}) copy-start(f32[4,4096]{1,0:T(4,128)} %param.8) | copy-start | bytes 196612
  7.2 208.1 %all-gather.2.cloned.1.call-start = ((), (), s32[]{:S(2)}) async-start(), calls=%async_computation.1 | async-start | bytes 10485760 | tf_op jit(solution)/shard_map/all_gather | solution.py:119
  9.1 21.5 %copy-start.3 = (bf16[2,16,4,4096]{3,2,1,0:T(4,128)(2,1)S(1)}, bf16[2,16,4,4096]{3,2,1,0:T(4,128)(2,1)}, u32[]{:S(2)}) copy-start(bf16[2,16,4,4096]{3,2,1,0:T(4,128)(2,1)} %param.7) | copy-start | bytes 3145732
  9.7 20.2 %collective-permute-start = (bf16[2,16,3,4096]{3,1,2,0:T(8,128)(2,1)S(1)}, bf16[2,16,3,4096]{3,1,2,0:T(8,128)(2,1)S(1)}, u32[]{:S(2)}, u32[]{:S(2)}) collective-permute-start(bf16[2,16,3,4096]{3,1,2,0:T(8,128)(2,1)S(1)} %copy.79), channel_id=1, source_target_pairs={{0,64},{64,128},{128,192},{1,65},{65,129},{129,193},{2,66},{66,130... | collective-permute-start | bytes 2359304 | tf_op jit(solution)/shard_map/ppermute | solution.py:20
  120.3 11.4 %copy-start.6 = (s32[256,1]{0,1:T(1,128)S(1)}, s32[256,1]{0,1:T(1,128)}, u32[]{:S(2)}) copy-start(s32[256,1]{0,1:T(1,128)} %param.11) | copy-start | bytes 3076
  131.6 1.8 copy-start.5
  131.6 2.2 copy-start.2
  242.0 3.6 %slice-start = ((s8[4718592]{0:T(1024)(128)(4,1)}), s8[4194304]{0:T(1024)(128)(4,1)S(1)}, s32[]{:S(2)}) async-start(s8[4718592]{0:T(1024)(128)(4,1)} %bitcast.99), calls=%async_computation.2 | async-start | bytes 8388608
  245.0 1.2 slice-start.1
  247.6 3.3 %copy-start.1 = (bf16[256,2,512]{2,1,0:T(2,128)(2,1)S(1)}, bf16[256,2,512]{2,1,0:T(2,128)(2,1)}, u32[]{:S(2)}) copy-start(bf16[256,2,512]{2,1,0:T(2,128)(2,1)} %param.10) | copy-start | bytes 1572868
Sparse Core Ops, SparseCore 0:
  131.8 83.4 all-gather.1
where the time goes:
time: 259 us; the launch traced here: 258 us
  waiting for transfers between devices  90.6 us (35%)
  local copies, waits for them, and re-layouts  85.5 us (33%)
  blocking collectives  41.3 us (16%)
  between operations  14.3 us (6%)
  matrix products  12.9 us (5%)
  other arithmetic  9 us (3%)
  starting transfers between devices  4.11 us (2%)
    all_gather x1, waiting for transfers between devices, shards(): lax.all_gather(shard_piece, 'section', axis=2, tiled=True)  74.9 us
    all_to_all x1, blocking collectives, shards(): lax.all_to_all(spectra, 'chan', split_axis=3, concat_axis=1, tiled=True)  41.3 us
    unnamed x22, local copies, waits for them, and re-layouts  22.1 us
    ppermute x1, waiting for transfers between devices, shifted(): return lax.ppermute(value, axis, pairs)  15.6 us
    convert_element_type x2, local copies, waits for them, and re-layouts, shards(): spectra = channelize(filtered.reshape(2, inputs_dev * frames_dev, NA * NB...  14.2 us
    all_to_all x1, local copies, waits for them, and re-layouts, shards(): lax.all_to_all(spectra, 'chan', split_axis=3, concat_axis=1, tiled=True)  11.4 us
    reshape x1, local copies, waits for them, and re-layouts, pair_products(): spectra.reshape(2, tile_count, TB, frame_count, channel_groups, AVG)  8.56 us
    reshape x1, local copies, waits for them, and re-layouts, pair_products(): jnp.transpose(blocks, (1, 4, 0, 2, 3, 5))  6.46 us
  transfers between devices with their start and end apart: 2, of which 2 were waited for; matrix products, arithmetic and copies ran while one was open for 4% of the time, Pallas kernels for 0%

commit v1 on v0

--- a/solution.py
+++ b/solution.py
@@ -116,7 +116,13 @@
     own_items = lax.dynamic_slice_in_dim(
         column_items, lax.axis_index("section") * items_dev, items_dev
     )
-    totals = pair_products(lax.all_gather(shard_piece, "section", axis=2, tiled=True), own_items)
+    build_slices_in = lambda incoming_x: jnp.concatenate(
+        jax.lax.all_to_all(
+            jnp.stack([incoming_x for _ in range(jax.lax.psum(1, "section"))]), "section", 0, 0
+        ),
+        axis=2,
+    )
+    totals = pair_products(build_slices_in(shard_piece), own_items)
     visibility = (totals * mean_factor)[None]
     return (visibility, beam_power)
 

time: 259 us -> 231 us (0.89)
  waiting for transfers between devices: 90.6 us -> 56.8 us
  between operations: 14.3 us -> 0.89 us
  local copies, waits for them, and re-layouts: 85.5 us -> 93.5 us
  starting transfers between devices: 4.11 us -> 9.27 us
  matrix products: 12.9 us -> 16.8 us
    all_gather x1 -> x0, waiting for transfers between devices: 74.9 us -> none  [shards(): lax.all_gather(shard_piece, 'section', axis=2, tiled=True)]
    all_to_all x0 -> x1, waiting for transfers between devices: none -> 41.2 us  [shards(): jax.lax.all_to_all(jnp.stack([incoming_x for _ in range(jax.lax.psum(1, '...]
    reshape x1, local copies, waits for them, and re-layouts: 8.56 us -> 2.63 us  [shards(): jnp.concatenate(jax.lax.all_to_all(jnp.stack([incoming_x for _ in range(j...]
    transpose x0 -> x1, local copies, waits for them, and re-layouts: none -> 5.41 us  [pair_products(): jnp.transpose(blocks, (1, 4, 0, 2, 3, 5))]
    another operation x1 -> x3, local copies, waits for them, and re-layouts: 3.5 us -> 8.86 us  [the longest x2 5.36 us: shards(): jnp.stack([incoming_x for _ in range(jax.lax.psum(1, 'section'))])]
    all_to_all x0 -> x1, starting transfers between devices: none -> 5.2 us  [shards(): jax.lax.all_to_all(jnp.stack([incoming_x for _ in range(jax.lax.psum(1, '...]
    dot_general x1, matrix products: 1.46 us -> 5.35 us  [pair_products(): lax.dot_general(row_block, col_block, numbers, preferred_element_type=jnp...]
    unnamed x22 -> x23, local copies, waits for them, and re-layouts: 22.1 us -> 25.7 us
where the time goes in v1:
time: 231 us; the launch traced here: 229 us
  local copies, waits for them, and re-layouts  93.5 us (40%)
  waiting for transfers between devices  56.8 us (25%)
  blocking collectives  41.3 us (18%)
  matrix products  16.8 us (7%)
  other arithmetic  10.5 us (5%)
  starting transfers between devices  9.27 us (4%)
    all_to_all x1, blocking collectives, shards(): lax.all_to_all(spectra, 'chan', split_axis=3, concat_axis=1, tiled=True)  41.3 us
    all_to_all x1, waiting for transfers between devices, shards(): jax.lax.all_to_all(jnp.stack([incoming_x for _ in range(jax.lax.psum(1, '...  41.2 us
    unnamed x23, local copies, waits for them, and re-layouts  25.7 us
    ppermute x1, waiting for transfers between devices, shifted(): return lax.ppermute(value, axis, pairs)  15.6 us
    convert_element_type x2, local copies, waits for them, and re-layouts, shards(): spectra = channelize(filtered.reshape(2, inputs_dev * frames_dev, NA * NB...  14.1 us
    all_to_all x1, local copies, waits for them, and re-layouts, shards(): lax.all_to_all(spectra, 'chan', split_axis=3, concat_axis=1, tiled=True)  10.6 us
    reshape x1, local copies, waits for them, and re-layouts, pair_products(): jnp.transpose(blocks, (1, 4, 0, 2, 3, 5))  6.72 us
    gather x1, local copies, waits for them, and re-layouts, pair_products(): jnp.take(tile_table, col_tiles * channel_groups + local_channel, axis=0)  5.9 us
  transfers between devices with their start and end apart: 2, of which 2 were waited for; matrix products, arithmetic and copies ran while one was open for 4% of the time, Pallas kernels for 0%

profile of v1, /device:TPU:1, one launch (start us, length us, event | category | flops | bytes accessed | tf_op | source)
XLA Modules:
  0.0 229.0 jit_solution(2958251105458405148)
XLA Ops:
  0.7 2.0 slice.54
  3.2 4.1 %collective-permute-start = (bf16[2,16,3,4096]{3,1,2,0:T(8,128)(2,1)S(1)}, bf16[2,16,3,4096]{3,1,2,0:T(8,128)(2,1)S(1)}, u32[]{:S(2)}, u32[]{:S(2)}) collective-permute-start(bf16[2,16,3,4096]{3,1,2,0:T(8,128)(2,1)S(1)} %copy.86), channel_id=1, source_target_pairs={{0,64},{64,128},{128,192},{1,65},{65,129},{129,193},{2,66},{66,130... | collective-permute-start | bytes 2359304 | tf_op jit(solution)/shard_map/ppermute | solution.py:20
  7.8 15.6 %collective-permute-done = bf16[2,16,3,4096]{3,1,2,0:T(8,128)(2,1)S(1)} collective-permute-done((bf16[2,16,3,4096]{3,1,2,0:T(8,128)(2,1)S(1)}, bf16[2,16,3,4096]{3,1,2,0:T(8,128)(2,1)S(1)}, u32[]{:S(2)}, u32[]{:S(2)}) %collective-permute-start) | collective-permute-done | bytes 786464 | tf_op jit(solution)/shard_map/ppermute | solution.py:20
  24.2 1.0 maximum_convert_fusion
  25.2 1.8 fusion.14
  27.0 3.4 %reshape_reshape.7 = f32[2,64,64,64]{3,2,1,0:T(8,128)} reshape(f32[2,16,4,4096]{3,2,1,0:T(4,128)S(1)} %fusion.14) | data formatting | bytes 4194304 | tf_op jit(solution)/shard_map/reshape;reshape | solution.py:35
  30.4 4.1 %fusion.10 = f32[2,64,64,64]{3,2,1,0:T(8,128)S(1)} fusion(f32[2,64,64,64]{3,2,1,0:T(8,128)} %reshape_reshape.7, f32[1,2,64,64]{2,3,0,1:T(8,128)S(1)} %get-tuple-element.27, f32[1,2,64,64]{2,3,0,1:T(8,128)S(1)} %get-tuple-element.26), kind=kOutput, calls=%fused_computation.18 | convolution fusion | flops 402669568 | bytes 4259840 | tf_op jit(solution)/shard_map/qmab,qrac->rmcb/dot_general | solution.py:36
  35.5 3.3 %fusion.13 = bf16[2,64,64,64]{3,2,1,0:T(8,128)(2,1)S(1)} fusion(f32[1,2,64,64]{2,3,0,1:T(8,128)S(1)} %get-tuple-element.27, f32[1,2,64,64]{2,3,0,1:T(8,128)S(1)} %get-tuple-element.26, f32[1,64,64,64]{3,2,1,0:T(8,128)S(1)} %get-tuple-element.21, f32[1,64,64,64]{3,2,1,0:T(8,128)S(1)} %get-tuple-element.20), kind=kOutput, calls=%fused_computation.19 | convolution fusion | flops 403718144 | bytes 3211264 | tf_op jit(solution)/shard_map/rmcb,rsbd->smdc/dot_general | solution.py:50
  38.8 2.2 convert_element_type.61
  41.0 12.0 %copy.59 = bf16[2,16,4,4096]{1,2,0,3:T(4,128)(2,1)} copy(bf16[2,16,4,4096]{3,2,1,0:T(4,128)(2,1)} %convert_element_type.61) | data formatting | bytes 2097152 | tf_op jit(solution)/shard_map/convert_element_type | solution.py:97
  53.0 11.9 %reshape.320 = bf16[64,2,4096]{2,1,0:T(2,128)(2,1)S(1)} reshape(bf16[4096,2,4,16]{3,2,1,0:T(4,128)(2,1)} %bitcast.105) | data formatting | bytes 2097152
  64.9 41.3 %all_to_all.20 = bf16[64,2,4096]{2,1,0:T(2,128)(2,1)S(1)} all-to-all(bf16[64,2,4096]{2,1,0:T(2,128)(2,1)S(1)} %reshape.320), channel_id=1, replica_groups=mesh['section'=4,'chan'=64] {'chan'}, dimensions={0} | all-to-all | bytes 2097152 | tf_op jit(solution)/shard_map/all_to_all | solution.py:101
  106.2 7.6 %reshape.321 = bf16[4096,2,4,16]{3,2,1,0:T(4,128)(2,1)} reshape(bf16[64,2,4096]{2,1,0:T(2,128)(2,1)S(1)} %all_to_all.20) | data formatting | bytes 2097152
  113.8 10.6 %copy.81 = bf16[2,16,4,64,64]{4,1,3,2,0:T(8,128)(2,1)S(1)} copy(bf16[2,16,4,64,64]{1,2,0,4,3:T(4,128)(2,1)} %bitcast.104) | data formatting | bytes 2097152 | tf_op jit(solution)/shard_map/all_to_all | solution.py:101
  124.4 1.6 copy.62
  126.0 3.7 %stack.62 = bf16[4,2,1024,4,64]{2,4,3,1,0:T(8,128)(2,1)} broadcast(bf16[2,1024,4,64]{1,3,2,0:T(8,128)(2,1)} %copy.62), dimensions={1,2,3,4} | broadcast | bytes 5242880 | tf_op jit(solution)/shard_map/stack | solution.py:121
  129.8 5.2 %all-to-all-start.1 = ((bf16[4,2,1024,4,64]{2,4,3,1,0:T(8,128)(2,1)}), bf16[4,2,1024,4,64]{2,4,3,1,0:T(8,128)(2,1)}, u32[]{:S(2)}, u32[]{:S(2)}) async-start(bf16[4,2,1024,4,64]{2,4,3,1,0:T(8,128)(2,1)} %stack.62), calls=%async_computation.1 | async-start | bytes 8388608 | tf_op jit(solution)/shard_map/all_to_all | solution.py:120
  135.0 1.7 gather_fusion
  137.2 3.5 %copy.70 = bf16[2,512,2,4,64]{1,4,3,2,0:T(8,128)(2,1)} copy(bf16[2,512,2,4,64]{4,2,1,3,0:T(2,128)(2,1)S(1)} %bitcast.108) | data formatting | bytes 2097152 | tf_op jit(solution)/shard_map/reshape.12
  140.7 2.0 convolution_bitcast_fusion
  143.6 41.2 %all-to-all-done.1 = bf16[4,2,1024,4,64]{2,4,3,1,0:T(8,128)(2,1)} async-done(((bf16[4,2,1024,4,64]{2,4,3,1,0:T(8,128)(2,1)}), bf16[4,2,1024,4,64]{2,4,3,1,0:T(8,128)(2,1)}, u32[]{:S(2)}, u32[]{:S(2)}) %all-to-all-start.1) | async-done | bytes 4194336 | tf_op jit(solution)/shard_map/all_to_all | solution.py:120
  184.7 2.6 %copy.63 = bf16[2,1024,4,4,64]{1,4,3,2,0:T(8,128)(2,1)S(1)} copy(bf16[2,1024,4,4,64]{1,4,3,0,2:T(8,128)(2,1)} %bitcast.26) | data formatting | bytes 8388608 | tf_op jit(solution)/shard_map/reshape | solution.py:119
  187.4 3.1 %copy.87 = bf16[256,8,8,128]{3,2,1,0:T(8,128)(2,1)} copy(bf16[256,8,8,128]{3,1,2,0:T(8,128)(2,1)S(1)} %bitcast.109) | data formatting | bytes 8388608
  190.4 6.7 %copy.65 = bf16[8,2,128,1024]{3,2,1,0:T(8,128)(2,1)} copy(bf16[8,2,128,1024]{2,0,3,1:T(8,128)(2,1)} %bitcast.102) | data formatting | bytes 8388608 | tf_op jit(solution)/shard_map/reshape | solution.py:69
  197.1 5.4 %copy.64 = bf16[8,1,2,128,16,64]{3,5,4,2,0,1:T(8,128)(2,1)} copy(bf16[8,1,2,128,16,64]{3,0,5,4,2,1:T(8,128)(2,1)} %bitcast.103) | data formatting | bytes 8388608 | tf_op jit(solution)/shard_map/transpose | solution.py:69
  202.5 5.8 %gather_fusion.1 = bf16[9,2,128,1024]{3,2,1,0:T(8,128)(2,1)} fusion(bf16[8,2,128,1024]{3,2,1,0:T(8,128)(2,1)} %copy.65, s32[1024]{0:T(1024)S(1)} %pad_clamp_fusion.2), kind=kCustom, calls=%fused_computation.clone | custom fusion | bytes 9437220 | tf_op jit(solution)/shard_map/jit(_take)/gather | solution.py:72
  208.3 2.9 %broadcast_select_fusion.1 = bf16[9,2,128,1024]{3,2,1,0:T(8,128)(2,1)S(1)} fusion(bf16[9,2,128,1024]{3,2,1,0:T(8,128)(2,1)} %gather_fusion.1, pred[9]{0:T(512)(128)(4,1)S(1)} %get-tuple-element.13), kind=kLoop, calls=%fused_computation.8 | loop fusion | flops 2359296 | bytes 9437193 | tf_op jit(solution)/shard_map/jit(_take)/select_n | solution.py:72
  211.2 1.9 fusion.54
  214.0 5.9 %gather_fusion.2 = bf16[9,2,128,1024]{2,3,1,0:T(8,128)(2,1)} fusion(bf16[8,2,128,1024]{2,3,1,0:T(8,128)(2,1)} %bitcast.106, s32[1024]{0:T(1024)S(1)} %pad_clamp_fusion.1), kind=kCustom, calls=%fused_computation.1.clone | custom fusion | bytes 9437220 | tf_op jit(solution)/shard_map/jit(_take)/gather | solution.py:73
  219.9 5.4 %fusion.20 = f32[1,9,1,128,128]{4,3,1,2,0:T(8,128)S(1)} fusion(bf16[9,2,128,1024]{3,2,1,0:T(8,128)(2,1)} %copy-done.2, bf16[9,2,128,1024]{2,3,1,0:T(8,128)(2,1)} %gather_fusion.2, pred[9]{0:T(512)(128)(4,1)S(1)} %get-tuple-element.16), kind=kOutput, calls=%fused_computation.32 | convolution fusion | flops 606339072 | bytes 10027017 | tf_op jit(solution)/shard_map/dot_general | solution.py:76
  225.8 2.0 fusion.21
  227.9 1.1 copy.71
  (37 shorter events, 5.6 us)
Async XLA Ops:
  0.6 134.4 %copy-start = (bf16[256,2,512]{2,1,0:T(2,128)(2,1)S(1)}, bf16[256,2,512]{2,1,0:T(2,128)(2,1)}, u32[]{:S(2)}) copy-start(bf16[256,2,512]{2,1,0:T(2,128)(2,1)} %param.10) | copy-start | bytes 1572868
  0.6 23.5 %copy-start.4 = (bf16[2,16,4,4096]{3,2,1,0:T(4,128)(2,1)S(1)}, bf16[2,16,4,4096]{3,2,1,0:T(4,128)(2,1)}, u32[]{:S(2)}) copy-start(bf16[2,16,4,4096]{3,2,1,0:T(4,128)(2,1)} %param.7) | copy-start | bytes 3145732
  0.7 7.1 %copy-start.6 = (f32[4,4096]{1,0:T(4,128)S(1)}, f32[4,4096]{1,0:T(4,128)}, u32[]{:S(2)}) copy-start(f32[4,4096]{1,0:T(4,128)} %param.8) | copy-start | bytes 196612
  3.2 20.2 %collective-permute-start = (bf16[2,16,3,4096]{3,1,2,0:T(8,128)(2,1)S(1)}, bf16[2,16,3,4096]{3,1,2,0:T(8,128)(2,1)S(1)}, u32[]{:S(2)}, u32[]{:S(2)}) collective-permute-start(bf16[2,16,3,4096]{3,1,2,0:T(8,128)(2,1)S(1)} %copy.86), channel_id=1, source_target_pairs={{0,64},{64,128},{128,192},{1,65},{65,129},{129,193},{2,66},{66,130... | collective-permute-start | bytes 2359304 | tf_op jit(solution)/shard_map/ppermute | solution.py:20
  129.8 5.2 %copy-start.8 = (s32[256,1]{0,1:T(1,128)S(1)}, s32[256,1]{0,1:T(1,128)}, u32[]{:S(2)}) copy-start(s32[256,1]{0,1:T(1,128)} %param.11) | copy-start | bytes 3076
  129.8 7.0 %copy-start.7 = (s32[1,36]{1,0:T(1,128)S(1)}, s32[1,36]{1,0:T(1,128)}, u32[]{:S(2)}) copy-start(s32[1,36]{1,0:T(1,128)} %param.9) | copy-start | bytes 436
  129.8 55.0 %all-to-all-start.1 = ((bf16[4,2,1024,4,64]{2,4,3,1,0:T(8,128)(2,1)}), bf16[4,2,1024,4,64]{2,4,3,1,0:T(8,128)(2,1)}, u32[]{:S(2)}, u32[]{:S(2)}) async-start(bf16[4,2,1024,4,64]{2,4,3,1,0:T(8,128)(2,1)} %stack.62), calls=%async_computation.1 | async-start | bytes 8388608 | tf_op jit(solution)/shard_map/all_to_all | solution.py:120
  211.2 2.8 %copy-start.2 = (bf16[9,2,128,1024]{3,2,1,0:T(8,128)(2,1)}, bf16[9,2,128,1024]{3,2,1,0:T(8,128)(2,1)S(1)}, u32[]{:S(2)}) copy-start(bf16[9,2,128,1024]{3,2,1,0:T(8,128)(2,1)S(1)} %broadcast_select_fusion.1) | copy-start | bytes 14155780
  219.9 5.4 %copy-start.3 = (bf16[9,2,128,1024]{2,3,1,0:T(8,128)(2,1)S(1)}, bf16[9,2,128,1024]{2,3,1,0:T(8,128)(2,1)}, u32[]{:S(2)}) copy-start(bf16[9,2,128,1024]{2,3,1,0:T(8,128)(2,1)} %gather_fusion.2) | copy-start | bytes 14155780
  219.9 5.9 %copy-start.5 = (bf16[9,1,128,1024]{3,2,1,0:T(8,128)(2,1)S(1)}, bf16[9,1,128,1024]{3,2,1,0:T(8,128)(2,1)}, u32[]{:S(2)}) copy-start(bf16[9,1,128,1024]{3,2,1,0:T(8,128)(2,1)} %get-tuple-element.19) | copy-start | bytes 7077892
  225.8 3.2 %copy-start.1 = (bf16[256,2,512]{2,1,0:T(2,128)(2,1)S(1)}, bf16[256,2,512]{2,1,0:T(2,128)(2,1)}, u32[]{:S(2)}) copy-start(bf16[256,2,512]{2,1,0:T(2,128)(2,1)} %param.10) | copy-start | bytes 1572868
